TPU v7x, 32 devices: a whole 2x2x4 slice. The times are simulated.
32 devices in a mesh: seq: 8 (over z, x), chan: 2 (over y), dp: 2 (over core).
Axes of the slice: x: 2, y: 2, z: 4, core: 2. Of those that a mesh axis runs over, the one named last changes fastest.
Arguments:
- ssm_input: bfloat16 [2, 1024, 4096], P('dp', 'seq', 'chan'), may hold values from -6 to 6
- gate_z: bfloat16 [2, 1024, 4096], P('dp', 'seq', 'chan'), may hold values from -6 to 6
- b_proj: bfloat16 [2, 1024, 128], P('dp', 'seq'), may hold values from -0.52734375 to 0.52734375
- c_proj: bfloat16 [2, 1024, 128], P('dp', 'seq'), may hold values from -6 to 6
- step_size: float32 [2, 1024, 64], P('dp', 'seq', 'chan'), may hold values from 0.02 to 0.2
- log_decay: float32 [2, 1024, 64], P('dp', 'seq', 'chan'), may hold values from -1 to 0, as said below
- skip_d: float32 [64], P('chan'), may hold values from 0.5 to 1.5
- norm_gain: float32 [4096], P('chan'), may hold values from 0.5 to 1.5
- w_out: bfloat16 [4096, 2048], P('chan'), may hold values from -0.09375 to 0.09375
- d_out: bfloat16 [2, 1024, 2048], P('dp', 'seq', 'chan'), may hold values from -6 to 6
- game_lengths: int32 [2, 4], P('dp'), may hold values from 1 to 512, 1024 in all within a row
Outputs:
- out: bfloat16 [2, 1024, 2048], P('dp', 'seq', 'chan')
- grad_x: bfloat16 [2, 1024, 4096], P('dp', 'seq', 'chan')
- grad_gain: float32 [4096], P('chan')
- grad_skip: float32 [64], P('chan')
Inputs may be any that keep to these rules, and one draw needn't show every extreme that they name: `game_lengths`: each row's 4 game lengths sum to 1024, and the longest is exactly 512. `log_decay`: a log decay per position and head.
All inputs are finite; a program needn't handle non-finite values.
Results may differ from a plain program's by a relative error of at most 0.017.
Values may be sent and summed in bfloat16 or wider, within the bound.
No kernel may reach another device: no remote copies, remote signals or barrier semaphores. Data moves between devices by JAX's collectives and lax.ppermute only.
A program may use at most 64 MiB of HBM per device.

v0:
```python
import jax
import jax.numpy as jnp
from jax import lax
from jax.sharding import PartitionSpec as P

NORM_EPS = 1e-05
PRECISE = lax.Precision.HIGHEST


def prefix(value, axis, join, neutral):
    count = lax.axis_size(axis)
    place = lax.axis_index(axis)
    ahead = count - 1 - place
    gathered = jax.tree.map(
        lambda a, kind: lax.all_gather(a.astype(kind), axis), value, (jnp.bfloat16, jnp.bfloat16)
    )
    state = jax.tree.map(lambda a, e: jnp.zeros_like(a) + jnp.asarray(e, a.dtype), value, neutral)

    def one(hop, state):
        source = count - 1 - hop
        return join(
            state,
            jax.tree.map(
                lambda a, own: lax.dynamic_index_in_dim(a, source, 0, False).astype(own.dtype),
                gathered,
                value,
            ),
        )

    return lax.fori_loop(0, ahead, one, state)


def block_parts(c_block, b_block, dt_block, decay_block, reset_block):
    block_len = c_block.shape[0]
    running = jnp.cumsum(decay_block, axis=0)
    reset_count = jnp.cumsum(reset_block, axis=0)
    scores = lax.dot_general(
        c_block, b_block, (((1,), (1,)), ((), ())), preferred_element_type=jnp.float32
    )
    indices = jnp.arange(block_len, dtype=jnp.int32)
    allowed = (indices[:, None] >= indices[None, :]) & (
        reset_count[:, None] == reset_count[None, :]
    )
    log_gap = running.T[:, :, None] - running.T[:, None, :]
    mixing = (
        jnp.where(allowed[None], jnp.exp(jnp.minimum(log_gap, 0.0)), 0.0)
        * scores[None]
        * dt_block.T[:, None, :]
    )
    mixing = mixing.astype(jnp.bfloat16)
    end_count = reset_count[-1]
    carry_weight = jnp.where((reset_count == 0)[:, None], jnp.exp(running), 0.0)
    tail_weight = jnp.where(
        (reset_count == end_count)[:, None], jnp.exp(running[-1][None, :] - running), 0.0
    )
    block_decay = jnp.where(end_count == 0, jnp.exp(running[-1]), 0.0)
    return (mixing, carry_weight, tail_weight, block_decay)


def chain_link(earlier, later):
    return (earlier[0] * later[0], later[0][:, None, None] * earlier[1] + later[1])


def local(
    ssm_input,
    gate_z,
    b_proj,
    c_proj,
    step_size,
    log_decay,
    skip_d,
    norm_gain,
    w_out,
    d_out,
    game_lengths,
):
    seq_len = ssm_input.shape[1]
    local_width = ssm_input.shape[2]
    heads_here = step_size.shape[2]
    head_dim = local_width // heads_here
    state_dim = b_proj.shape[2]
    block_len = min(512, seq_len)
    count_blocks = seq_len // block_len
    total_width = local_width * lax.axis_size("chan")
    x_heads = ssm_input[0].reshape(seq_len, heads_here, head_dim)
    c_rows = c_proj[0]
    b_rows = b_proj[0]
    dt_rows = step_size[0]
    lengths = game_lengths[0]
    starts = jnp.cumsum(lengths) - lengths
    sequence_positions = lax.axis_index("seq") * seq_len + jnp.arange(seq_len, dtype=jnp.int32)
    resets = jnp.any(sequence_positions[:, None] == starts[None, :], axis=1).astype(jnp.int32)

    def blocked(array):
        return array.reshape((count_blocks, block_len) + array.shape[1:])

    zero_state = jnp.zeros((heads_here, state_dim, head_dim), jnp.float32)
    unit_decay = jnp.ones((heads_here,), jnp.float32)

    def forward_step(state_pair, block_inputs):
        local_state, before = state_pair
        x_block, c_block, b_block, dt_block, decay_block, reset_block = block_inputs
        mixing, carry_weight, tail_weight, block_decay = block_parts(
            c_block, b_block, dt_block, decay_block, reset_block
        )
        inside = jnp.einsum("hts,shp->thp", mixing, x_block, preferred_element_type=jnp.float32)
        carried = carry_weight[:, :, None] * jnp.einsum(
            "tn,hnp->thp", c_block.astype(jnp.float32), local_state, precision=PRECISE
        )
        scaled = ((tail_weight * dt_block)[:, :, None] * x_block).astype(jnp.bfloat16)
        fresh_state = jnp.einsum("sn,shp->hnp", b_block, scaled, preferred_element_type=jnp.float32)
        new_pair = (block_decay[:, None, None] * local_state + fresh_state, before * block_decay)
        return (
            new_pair,
            (
                inside + carried,
                carry_weight * before[None, :],
                mixing,
                carry_weight,
                tail_weight,
                block_decay,
            ),
        )

    forward_inputs = (
        blocked(x_heads),
        blocked(c_rows),
        blocked(b_rows),
        blocked(dt_rows),
        blocked(log_decay[0]),
        blocked(resets),
    )
    (dev_state, dev_decay), (
        ssd_blocks,
        incoming_weight,
        mixings,
        carry_weights,
        tail_weights,
        block_decays,
    ) = lax.scan(forward_step, (zero_state, unit_decay), forward_inputs)
    decays = lax.all_gather(dev_decay[None, :], "seq", axis=0, tiled=True)
    my_index = lax.axis_index("seq")
    device_ids = jnp.arange(decays.shape[0], dtype=jnp.int32)
    between = (device_ids[None, :] > device_ids[:, None]) & (device_ids[None, :] < my_index)
    weights = jnp.prod(jnp.where(between[:, :, None], decays[None, :, :], 1.0), axis=1)
    weights = weights * (device_ids < my_index).astype(jnp.float32)[:, None]
    incoming = zero_state + jnp.einsum(
        "mh,mhnp->hnp",
        weights,
        lax.all_gather(dev_state[None].astype(jnp.bfloat16), "seq", axis=0, tiled=True).astype(
            jnp.float32
        ),
        precision=PRECISE,
    )
    from_left = jnp.einsum("tn,hnp->thp", c_rows.astype(jnp.float32), incoming, precision=PRECISE)
    ssd_out = (
        ssd_blocks.reshape(seq_len, heads_here, head_dim)
        + incoming_weight.reshape(seq_len, heads_here)[:, :, None] * from_left
    )
    ssd_out = ssd_out + skip_d[None, :, None] * x_heads.astype(jnp.float32)
    gate_act = jax.nn.silu(gate_z[0].astype(jnp.float32))
    gated = ssd_out.reshape(seq_len, local_width) * gate_act
    square_total = lax.psum(jnp.sum(gated * gated, axis=1), "chan")
    inv_rms = lax.rsqrt(square_total / total_width + NORM_EPS)
    normed = (gated * norm_gain).astype(jnp.bfloat16)
    w_cols = w_out
    projected = (
        lax.psum_scatter(
            lax.dot_general(
                w_cols, normed, (((0,), (1,)), ((), ())), preferred_element_type=jnp.float32
            ).astype(jnp.bfloat16),
            "chan",
            scatter_dimension=0,
            tiled=True,
        )
        .astype(jnp.float32)
        .T
    )
    out = (inv_rms[:, None] * projected).astype(jnp.bfloat16)[None]
    cotangent = d_out[0]
    w_cols = w_out
    pulled = lax.dot_general(
        lax.all_gather(cotangent, "chan", axis=1, tiled=True),
        w_cols,
        (((1,), (1,)), ((), ())),
        preferred_element_type=jnp.float32,
    )
    out_dot = lax.psum(jnp.sum(normed.astype(jnp.float32) * pulled, axis=1), "chan")
    d_normed = inv_rms[:, None] * pulled
    gain_local = jnp.sum(gated * d_normed, axis=0)
    d_ssd = (
        (norm_gain * d_normed - (inv_rms**3 * out_dot / total_width)[:, None] * gated) * gate_act
    ).astype(jnp.bfloat16)
    d_heads = d_ssd.reshape(seq_len, heads_here, head_dim)
    skip_local = jnp.sum(d_heads.astype(jnp.float32) * x_heads.astype(jnp.float32), axis=(0, 2))
    grad_gain, grad_skip = lax.psum((gain_local, skip_local), ("seq", "dp"))

    def backward_step(state_pair, block_inputs):
        local_adjoint, later_decay = state_pair
        d_block, c_block, b_block, dt_block, mixing, carry_weight, tail_weight, block_decay = (
            block_inputs
        )
        inside = jnp.einsum("hts,thp->shp", mixing, d_block, preferred_element_type=jnp.float32)
        carried = (dt_block * tail_weight)[:, :, None] * jnp.einsum(
            "sn,hnp->shp", b_block.astype(jnp.float32), local_adjoint, precision=PRECISE
        )
        weighted = (carry_weight[:, :, None] * d_block).astype(jnp.bfloat16)
        fresh_adjoint = jnp.einsum(
            "tn,thp->hnp", c_block, weighted, preferred_element_type=jnp.float32
        )
        new_pair = (
            fresh_adjoint + block_decay[:, None, None] * local_adjoint,
            later_decay * block_decay,
        )
        return (new_pair, (inside + carried, dt_block * tail_weight * later_decay[None, :]))

    backward_inputs = (
        blocked(d_heads),
        blocked(c_rows),
        blocked(b_rows),
        blocked(dt_rows),
        mixings,
        carry_weights,
        tail_weights,
        block_decays,
    )
    (dev_adjoint, _), (grad_blocks, outgoing_weight) = lax.scan(
        backward_step, (zero_state, unit_decay), backward_inputs, reverse=True
    )
    _, from_right = prefix((dev_decay, dev_adjoint), "seq", chain_link, (unit_decay, zero_state))
    right_terms = jnp.einsum(
        "sn,hnp->shp", b_rows.astype(jnp.float32), from_right, precision=PRECISE
    )
    grad_heads = (
        grad_blocks.reshape(seq_len, heads_here, head_dim)
        + outgoing_weight.reshape(seq_len, heads_here)[:, :, None] * right_terms
    )
    grad_heads = grad_heads + skip_d[None, :, None] * d_heads.astype(jnp.float32)
    grad_x = grad_heads.astype(jnp.bfloat16).reshape(1, seq_len, local_width)
    return (out, grad_x, grad_gain, grad_skip)


def solution(mesh):
    return jax.shard_map(
        local,
        mesh=mesh,
        in_specs=(
            P("dp", "seq", "chan"),
            P("dp", "seq", "chan"),
            P("dp", "seq", None),
            P("dp", "seq", None),
            P("dp", "seq", "chan"),
            P("dp", "seq", "chan"),
            P("chan"),
            P("chan"),
            P("chan", None),
            P("dp", "seq", "chan"),
            P("dp", None),
        ),
        out_specs=(P("dp", "seq", "chan"), P("dp", "seq", "chan"), P("chan"), P("chan")),
        check_vma=False,
    )
```

profile of v0, /device:TPU:0, one launch (start us, length us, event | category | flops | bytes accessed | tf_op | source)
XLA Modules:
  0.0 248.1 jit_solution(2390316497509367646)
XLA Ops:
  18.2 22.6 %all-gather.3 = f32[8,1,32]{2,1,0:T(1,128)S(1)} all-gather(f32[1,1,32]{2,1,0:T(1,128)S(1)} %get-tuple-element.227), channel_id=1, replica_groups=mesh['seq'=8,'chan'=2,'dp'=2] {'seq'}, dimensions={0}, use_global_device_ids=true | all-gather | bytes 1152 | tf_op jit(solution)/shard_map/all_gather | solution.py:141
  40.9 7.1 %all-gather.1 = bf16[1,128,2048]{2,1,0:T(8,128)(2,1)} all-gather(bf16[1,128,1024]{2,1,0:T(8,128)(2,1)S(1)} %copy-done.7), channel_id=3, replica_groups=mesh['seq'=8,'chan'=2,'dp'=2] {'chan'}, dimensions={2}, use_global_device_ids=true | all-gather | bytes 786432 | tf_op jit(solution)/shard_map/all_gather | solution.py:183
  48.4 2.1 convolution_bitcast_fusion.5
  51.1 40.1 %all-gather.8.cloned.1.call-done = bf16[256,128,64]{1,2,0:T(8,128)(2,1)} async-done(((bf16[32,128,64]{1,2,0:T(8,128)(2,1)}), bf16[256,128,64]{1,2,0:T(8,128)(2,1)}) %all-gather.8.cloned.1.call-update) | async-done | bytes 4194320 | tf_op jit(solution)/shard_map/all_gather | solution.py:150
  91.1 3.2 %multiply_reduce_fusion = f32[32,128,64]{1,2,0:T(8,128)S(1)} fusion(bf16[32,8,128,64]{2,3,0,1:T(8,128)(2,1)} %bitcast.158, f32[32,8]{0,1:T(8,128)S(1)} %multiply_bitcast_fusion), kind=kLoop, calls=%fused_computation.3 | loop fusion | flops 6029312 | bytes 5243904 | tf_op jit(solution)/shard_map/mh,mhnp->hnp/dot_general | solution.py:147
  94.4 1.9 multiply_reduce_fusion.3
  96.3 1.6 copy.91
  97.9 4.9 %psum.28 = f32[128]{0:T(128)S(1)} all-reduce(f32[128]{0:T(128)S(1)} %get-tuple-element.232), channel_id=1, replica_groups=mesh['seq'=8,'chan'=2,'dp'=2] {'chan'}, use_global_device_ids=true, to_apply=%region_6.7 | all-reduce | flops 128 | bytes 1024 | tf_op jit(solution)/shard_map/psum | solution.py:163
  102.9 5.6 %fusion = bf16[2048,128]{0,1:T(8,128)(2,1)} fusion(bf16[2048,2048]{1,0:T(8,128)(2,1)} %param.21, f32[2048]{0:T(1024)S(1)} %copy-done.9, f32[128,2048]{1,0:T(8,128)S(1)} %copy.91, bf16[1,128,2048]{2,1,0:T(8,128)(2,1)S(1)} %copy-done.3), kind=kOutput, calls=%fused_computation.5 | convolution fusion | flops 1076101120 | bytes 10493952 | tf_op jit(solution)/shard_map/dot_general | solution.py:169
  108.4 7.6 %multiply_reduce_fusion.1 = (f32[2048]{0:T(1024)S(1)}, f32[128]{0:T(128)S(1)}, f32[128,2048]{1,0:T(8,128)}) fusion(f32[128]{0:T(128)S(1)} %add_rsqrt_fusion, f32[128,2048]{1,0:T(8,128)S(1)} %copy.91, bf16[1,128,2048]{2,1,0:T(8,128)(2,1)S(1)} %copy-done.3, f32[2048]{0:T(1024)S(1)} %copy-done.9, bf16[2048,2048]{1,0:T(8,128)(2,1)} %param.21, ...), kind=kOutput, calls=%fused_computation.42 | convolution fusion | flops 1077409664 | bytes 11551744 | tf_op jit(solution)/shard_map/dot_general | solution.py:182
  116.0 4.9 %psum.29 = f32[128]{0:T(128)S(1)} all-reduce(f32[128]{0:T(128)S(1)} %get-tuple-element.210), channel_id=1, replica_groups=mesh['seq'=8,'chan'=2,'dp'=2] {'chan'}, use_global_device_ids=true, to_apply=%region_9.10 | all-reduce | flops 128 | bytes 1024 | tf_op jit(solution)/shard_map/psum | solution.py:188
  121.0 2.1 fusion.18
  124.6 18.1 %all-gather.4 = bf16[8,1,32]{2,1,0:T(2,128)(2,1)S(1)} all-gather(bf16[1,1,32]{2,1,0:T(2,128)(2,1)S(1)} %get-tuple-element.225), channel_id=1, replica_groups=mesh['seq'=8,'chan'=2,'dp'=2] {'seq'}, dimensions={0}, use_global_device_ids=true | all-gather | bytes 576 | tf_op jit(solution)/shard_map/all_gather | solution.py:15
  143.2 33.1 %all-reduce = (f32[2048]{0:T(1024)}, f32[32]{0:T(128)}) all-reduce(f32[2048]{0:T(1024)S(1)} %get-tuple-element.209, f32[32]{0:T(128)S(1)} %reduce_sum.48), channel_id=1, replica_groups=mesh['seq'=8,'chan'=2,'dp'=2] {'seq','dp'}, use_global_device_ids=true, to_apply=%region_13.14 | all-reduce | flops 2080 | bytes 16640 | tf_op jit(solution)/shard_map/psum | solution.py:196
  177.0 1.6 fusion.4
  178.6 1.8 fusion.26
  180.4 29.6 %all-gather.10.cloned.1.call-done = bf16[256,128,64]{1,2,0:T(8,128)(2,1)} async-done(((bf16[32,128,64]{1,2,0:T(8,128)(2,1)}), bf16[256,128,64]{1,2,0:T(8,128)(2,1)}) %all-gather.10.cloned.1.call-update) | async-done | bytes 4194320 | tf_op jit(solution)/shard_map/all_gather | solution.py:15
  210.2 27.1 %while.9 = (s32[]{:T(128)}, f32[32,128,64]{2,1,0:T(8,128)S(1)}, s32[]{:T(128)}, bf16[8,32]{1,0:T(8,128)(2,1)S(1)}, bf16[8,32,128,64]{2,3,1,0:T(8,128)(2,1)}, /*index=5*/s32[]{:T(128)}, s32[]{:T(128)}, s32[]{:T(128)}, s32[]{:T(128)}) while((s32[]{:T(128)}, f32[32,128,64]{2,1,0:T(8,128)S(1)}, s32[]{:T(128)}, bf16[8,32]{1,0:T(8,128)(2,1)S(1)}, ...), condition=%wide.region_11.12_spmd, body=%wide.region_10.11_spmd.sunk | while | flops 786470 | bytes 4719059 | solution.py:30
  210.2 1.9 constant_dynamic-slice_fusion.2
  212.1 1.5 copy.114
  214.1 1.9 constant_dynamic-slice_fusion.2
  215.9 1.5 copy.114
  217.9 1.9 constant_dynamic-slice_fusion.2
  219.8 1.5 copy.114
  221.8 1.9 constant_dynamic-slice_fusion.2
  223.7 1.5 copy.114
  225.7 1.9 constant_dynamic-slice_fusion.2
  227.5 1.5 copy.114
  229.5 1.9 constant_dynamic-slice_fusion.2
  233.4 1.9 constant_dynamic-slice_fusion.2
  235.3 1.5 copy.114
  237.3 3.2 %fusion.13 = bf16[128,32,64]{0,2,1:T(8,128)(2,1)S(1)} fusion(f32[128,32,64]{0,2,1:T(8,128)} %fusion.4, f32[32,128,64]{2,1,0:T(8,128)S(1)} %get-tuple-element.172, bf16[128,32,64]{0,2,1:T(8,128)(2,1)} %bitcast.162, f32[32]{0:T(128)S(1)} %copy-done.10, f32[128,32]{0,1:T(8,128)S(1)} %copy.87, bf16[1,128,128]{2,1,0:T(8,128)(2,1)S(1)} %copy-done.5), kind=kOutput, calls=%fused_computation.31 | convolution fusion | flops 404226048 | bytes 3195008 | tf_op jit(solution)/shard_map/sn,hnp->shp/dot_general | solution.py:231
  (92 shorter events, 19.9 us)
Async XLA Ops:
  7.2 41.1 %copy-start = (bf16[1,128,128]{2,1,0:T(8,128)(2,1)S(1)}, bf16[1,128,128]{2,1,0:T(8,128)(2,1)}, u32[]{:S(2)}) copy-start(bf16[1,128,128]{2,1,0:T(8,128)(2,1)} %param.16) | copy-start | bytes 98308
  7.2 6.4 %copy-start.1 = (bf16[1,128,2048]{2,1,0:T(8,128)(2,1)S(1)}, bf16[1,128,2048]{2,1,0:T(8,128)(2,1)}, u32[]{:S(2)}) copy-start(bf16[1,128,2048]{2,1,0:T(8,128)(2,1)} %param.13) | copy-start | bytes 1572868
  7.2 84.0 %all-gather.8.cloned.1.call-start = ((), (), s32[]{:S(2)}) async-start(), calls=%async_computation.2 | async-start | bytes 4718592 | tf_op jit(solution)/shard_map/all_gather | solution.py:150
  13.6 0.8 copy-start.5
  13.7 2.9 %copy-start.3 = (bf16[1,128,2048]{2,1,0:T(8,128)(2,1)S(1)}, bf16[1,128,2048]{2,1,0:T(8,128)(2,1)}, u32[]{:S(2)}) copy-start(bf16[1,128,2048]{2,1,0:T(8,128)(2,1)} %param.14) | copy-start | bytes 1572868
  15.4 163.2 %reduce-scatter.2.cloned.1.call-start = ((), (), s32[]{:S(2)}) async-start(), calls=%async_computation.1 | async-start | bytes 786432 | tf_op jit(solution)/shard_map/reduce_scatter | solution.py:168
  16.6 24.3 %copy-start.7 = (bf16[1,128,1024]{2,1,0:T(8,128)(2,1)S(1)}, bf16[1,128,1024]{2,1,0:T(8,128)(2,1)}, u32[]{:S(2)}) copy-start(bf16[1,128,1024]{2,1,0:T(8,128)(2,1)} %param.22) | copy-start | bytes 786436
  17.8 30.6 %copy-start.8 = (f32[1,128,32]{1,2,0:T(8,128)S(1)}, f32[1,128,32]{1,2,0:T(8,128)}, u32[]{:S(2)}) copy-start(f32[1,128,32]{1,2,0:T(8,128)} %param.17) | copy-start | bytes 49156
  91.1 3.3 %copy-start.4 = (f32[1,128,2048]{1,2,0:T(8,128)S(1)}, f32[1,128,2048]{1,2,0:T(8,128)}, u32[]{:S(2)}) copy-start(f32[1,128,2048]{1,2,0:T(8,128)} %copy.90) | copy-start | bytes 3145732
  91.1 3.3 %copy-start.6 = (bf16[1,128,2048]{1,2,0:T(8,128)(2,1)S(1)}, bf16[1,128,2048]{1,2,0:T(8,128)(2,1)}, u32[]{:S(2)}) copy-start(bf16[1,128,2048]{1,2,0:T(8,128)(2,1)} %copy.84) | copy-start | bytes 1572868
  91.1 3.3 %copy-start.10 = (f32[32]{0:T(128)S(1)}, f32[32]{0:T(128)}, u32[]{:S(2)}) copy-start(f32[32]{0:T(128)} %param.19) | copy-start | bytes 388
  96.3 6.5 %copy-start.9 = (f32[2048]{0:T(1024)S(1)}, f32[2048]{0:T(1024)}, u32[]{:S(2)}) copy-start(f32[2048]{0:T(1024)} %param.20) | copy-start | bytes 24580
  121.0 89.0 %all-gather.10.cloned.1.call-start = ((), (), s32[]{:S(2)}) async-start(), calls=%async_computation.3 | async-start | bytes 4718592 | tf_op jit(solution)/shard_map/all_gather | solution.py:15
  143.0 67.0 %copy-start.2 = (bf16[128,2048]{0,1:T(8,128)(2,1)}, bf16[128,2048]{0,1:T(8,128)(2,1)S(1)}, u32[]{:S(2)}) copy-start(bf16[128,2048]{0,1:T(8,128)(2,1)S(1)} %copy.92) | copy-start | bytes 1572868
Sparse Core Ops, SparseCore 0:
  15.6 75.5 all-gather.7
  121.1 13.1 reduce-scatter.1
  136.4 73.4 all-gather.9
where the time goes:
time: 249 us; the launch traced here: 248 us
  blocking collectives  90.7 us (36%)
  waiting for transfers between devices  69.7 us (28%)
  local copies, waits for them, and re-layouts  33.3 us (13%)
  matrix products  25.7 us (10%)
  between operations  14.7 us (6%)
  other arithmetic  13.6 us (5%)
    all_gather x1, waiting for transfers between devices, local(): lax.all_gather(dev_state[None].astype(jnp.bfloat16), 'seq', axis=0, tiled...  40.1 us
    psum x1, blocking collectives, local(): grad_gain, grad_skip = lax.psum((gain_local, skip_local), ('seq', 'dp'))  33.1 us
    all_gather x1, waiting for transfers between devices, prefix(): lax.all_gather(a.astype(kind), axis)  29.6 us
    dynamic_slice x14, local copies, waits for them, and re-layouts, one(): lax.dynamic_index_in_dim(a, source, 0, False).astype(own.dtype)  23.7 us
    all_gather x1, blocking collectives, local(): decays = lax.all_gather(dev_decay[None, :], 'seq', axis=0, tiled=True)  22.6 us
    all_gather x1, blocking collectives, prefix(): lax.all_gather(a.astype(kind), axis)  18.1 us
    dot_general x1, matrix products, local(): lax.dot_general(lax.all_gather(cotangent, 'chan', axis=1, tiled=True), w_...  7.57 us
    all_gather x1, blocking collectives, local(): lax.all_gather(cotangent, 'chan', axis=1, tiled=True)  7.15 us
  transfers between devices with their start and end apart: 3, of which 2 were waited for; matrix products, arithmetic and copies ran while one was open for 6% of the time, Pallas kernels for 0%

commit v1 on v0

v1 whole, which is shorter than its diff:
```python
import functools

import jax
import jax.numpy as jnp
from jax import lax
from jax.experimental import pallas as pl
from jax.experimental.pallas import tpu as pltpu
from jax.sharding import PartitionSpec as P

NORM_EPS = 1e-05
PRECISE = lax.Precision.HIGHEST
LANES = 128
F32 = jnp.float32
BF16 = jnp.bfloat16
VMEM = pl.BlockSpec(memory_space=pltpu.VMEM)
SMEM = pl.BlockSpec(memory_space=pltpu.SMEM)


def call(body, shapes, specs, scratch=()):
    return pl.pallas_call(
        body,
        out_shape=[jax.ShapeDtypeStruct(s, d) for s, d in shapes],
        in_specs=list(specs),
        out_specs=[VMEM] * len(shapes),
        scratch_shapes=list(scratch),
        name=body.__name__ if hasattr(body, "__name__") else body.func.__name__,
    )


def dot(a, b, da, db, precision=None):
    return lax.dot_general(
        a, b, (((da,), (db,)), ((), ())), precision=precision, preferred_element_type=F32
    )


def tile(width, index):
    return pl.ds(index * width, width)


def spread(weights, index, head_dim):
    per = LANES // head_dim
    rows = weights.shape[0]
    lane = lax.broadcasted_iota(jnp.int32, (rows, LANES), 1)
    result = jnp.broadcast_to(weights[:, index * per : index * per + 1], (rows, LANES))
    for k in range(1, per):
        column = weights[:, index * per + k : index * per + k + 1]
        result = jnp.where(lane >= k * head_dim, column, result)
    return result


def counts(lengths, offset, position):
    total = jnp.zeros(position.shape, jnp.int32)
    start = jnp.int32(0)
    for game in range(lengths.shape[1]):
        local = start - offset
        total = total + jnp.where((position >= local) & (local >= 0), 1, 0)
        start = start + lengths[0, game]
    return total


def triangle(n, upper):
    row = lax.broadcasted_iota(jnp.int32, (n, n), 0)
    col = lax.broadcasted_iota(jnp.int32, (n, n), 1)
    return jnp.where((row <= col) if upper else (row >= col), 1.0, 0.0).astype(F32)


def state_kernel(x, b, dt, decay, lengths, offset, payload, carry, tail, scaled, *, head_dim):
    n, heads = dt.shape
    width = x.shape[1]
    running = dot(triangle(n, False), decay[...], 1, 0, PRECISE)
    position = lax.broadcasted_iota(jnp.int32, (n, 1), 0)
    count = counts(lengths, offset[0], position)
    end = counts(lengths, offset[0], jnp.full((1, 1), n - 1, jnp.int32))
    last = running[n - 1 : n, :]
    carry[...] = jnp.where(count == 0, jnp.exp(running), 0.0)
    tails = jnp.where(count == end, jnp.exp(last - running), 0.0) * dt[...]
    tail[...] = tails
    for i in range(width // LANES):
        at = tile(LANES, i)
        scaled[:, at] = (spread(tails, i, head_dim) * x[:, at].astype(F32)).astype(BF16)
    payload[:, :width] = dot(b[...], scaled[...], 0, 0).astype(BF16)
    total = jnp.where(end == 0, jnp.exp(last), 0.0)
    high = total.astype(BF16).astype(F32)
    low = total - high
    row = lax.broadcasted_iota(jnp.int32, (heads, LANES), 0)
    col = lax.broadcasted_iota(jnp.int32, (heads, LANES), 1)
    extra = dot(high, jnp.where(row == col, 1.0, 0.0).astype(F32), 1, 0, PRECISE)
    extra = extra + dot(low, jnp.where(row + heads == col, 1.0, 0.0).astype(F32), 1, 0, PRECISE)
    payload[:, width:] = jnp.broadcast_to(extra, (payload.shape[0], LANES)).astype(BF16)


def mixing_kernel(x, b, c, dt, decay, lengths, offset, mixing, inside, *, head_dim):
    n, heads = dt.shape
    width = x.shape[1]
    per = LANES // head_dim
    running = dot(triangle(n, False), decay[...], 1, 0, PRECISE)
    across = dot(decay[...], triangle(n, True), 0, 0, PRECISE)
    t = lax.broadcasted_iota(jnp.int32, (n, n), 0)
    s = lax.broadcasted_iota(jnp.int32, (n, n), 1)
    same = counts(lengths, offset[0], t) == counts(lengths, offset[0], s)
    scores = jnp.where((t >= s) & same, dot(c[...], b[...], 1, 1), 0.0)
    lane = lax.broadcasted_iota(jnp.int32, (n, LANES), 1) // head_dim
    steps = dt[...]
    for i in range(width // LANES):
        at = tile(LANES, i)
        stepped = spread(steps, i, head_dim) * x[:, at].astype(F32)
        total = jnp.zeros((n, LANES), F32)
        for k in range(per):
            h = i * per + k
            gap = running[:, h : h + 1] - across[h : h + 1, :]
            mixed = (jnp.exp(jnp.minimum(gap, 0.0)) * scores).astype(BF16)
            mixing[h] = mixed
            total = total + dot(mixed, jnp.where(lane == k, stepped, 0.0).astype(BF16), 1, 0)
        inside[:, at] = total


def onward_kernel(parts, states, decays, *, heads, head_dim):
    count = parts.shape[0]
    width = states.shape[2]
    row = lax.broadcasted_iota(jnp.int32, (LANES, width), 0)
    col = lax.broadcasted_iota(jnp.int32, (LANES, width), 1) // head_dim
    pick = jnp.where((row == col) | (row == col + heads), 1.0, 0.0).astype(BF16)
    own = jnp.concatenate([parts[m, 0:1, width:] for m in range(count)], axis=0)
    spreads = dot(own, pick, 1, 0)
    decays[...] = spreads
    state = jnp.zeros(states.shape[1:], F32)
    states[0] = state.astype(BF16)
    for m in range(count - 1):
        state = spreads[m : m + 1, :] * state + parts[m, :, :width].astype(F32)
        states[m + 1] = state.astype(BF16)


def backward_kernel(parts, decays, states, sums):
    count = parts.shape[0]
    width = states.shape[2]
    state = jnp.zeros(states.shape[1:], F32)
    states[count - 1] = state.astype(BF16)
    for m in range(count - 1, 0, -1):
        state = decays[m : m + 1, :] * state + parts[m, :, :width].astype(F32)
        states[m - 1] = state.astype(BF16)
    total = parts[0, :, width:].astype(F32)
    for m in range(1, count):
        total = total + parts[m, :, width:].astype(F32)
    sums[...] = total


def gated_kernel(c, incoming, inside, carry, x, z, skip, gain, pulled, gated, normed, stats, *, head_dim):
    n, width = x.shape
    per = LANES // head_dim
    carries = carry[...]
    lane = lax.broadcasted_iota(jnp.int32, (1, LANES), 1)
    squares = jnp.zeros((n, LANES), F32)
    products = jnp.zeros((n, LANES), F32)
    for i in range(width // LANES):
        at = tile(LANES, i)
        skips = jnp.full((1, LANES), skip[i * per], F32)
        for k in range(1, per):
            skips = jnp.where(lane >= k * head_dim, skip[i * per + k], skips)
        left = dot(c[...], incoming[:, at], 1, 0)
        ssd = inside[:, at] + spread(carries, i, head_dim) * left + skips * x[:, at].astype(F32)
        gate = z[:, at].astype(F32)
        value = ssd * (gate / (1.0 + jnp.exp(-gate)))
        gated[:, at] = value
        scaled = (value * gain[:, at]).astype(BF16)
        normed[:, at] = scaled
        squares = squares + value * value
        products = products + scaled.astype(F32) * pulled[:, at]
    first = jnp.sum(squares, axis=1, keepdims=True)
    second = jnp.sum(products, axis=1, keepdims=True)
    lanes = lax.broadcasted_iota(jnp.int32, (n, LANES), 1)
    both = jnp.where(lanes == 0, first, second)
    stats[...] = both.T[: stats.shape[0], :]


def cotangent_kernel(
    stats, c, carry, x, z, gain, pulled, gated, d_ssd, payload, inverse, weighted, sums, *, head_dim, total, rows
):
    n, width = x.shape
    folded = jnp.concatenate([stats[...]] * (LANES // stats.shape[0]), axis=0).T
    inv = lax.rsqrt(folded[:, 0:1] / total + NORM_EPS)
    inverse[...] = inv
    factor = inv * inv * inv * folded[:, 1:2] / total
    carries = carry[...]
    tiles = width // LANES
    for i in range(tiles):
        at = tile(LANES, i)
        gate = z[:, at].astype(F32)
        act = gate / (1.0 + jnp.exp(-gate))
        value = gated[:, at]
        d_normed = inv * pulled[:, at]
        d_own = ((gain[:, at] * d_normed - factor * value) * act).astype(BF16)
        d_ssd[:, at] = d_own
        d_wide = d_own.astype(F32)
        weighted[:, at] = (spread(carries, i, head_dim) * d_wide).astype(BF16)
        sums[i : i + 1, :LANES] = jnp.sum(value * d_normed, axis=0, keepdims=True)
        sums[i : i + 1, LANES:] = jnp.sum(d_wide * x[:, at].astype(F32), axis=0, keepdims=True)
    payload[:, :width] = dot(c[...], weighted[...], 0, 0).astype(BF16)
    pieces = sums[...].astype(BF16)
    for j in range(payload.shape[0] // rows):
        payload[j * rows : (j + 1) * rows, width:] = pieces


def inside_kernel(mixing, d_ssd, dt, skip, inside, *, head_dim):
    n, width = d_ssd.shape
    per = LANES // head_dim
    steps = dt[...]
    lane = lax.broadcasted_iota(jnp.int32, (n, LANES), 1)
    for i in range(width // LANES):
        at = tile(LANES, i)
        d_own = d_ssd[:, at]
        skips = jnp.full((n, LANES), skip[i * per], F32)
        total = dot(mixing[i * per], d_own, 0, 0)
        for k in range(1, per):
            skips = jnp.where(lane >= k * head_dim, skip[i * per + k], skips)
            total = jnp.where(lane >= k * head_dim, dot(mixing[i * per + k], d_own, 0, 0), total)
        inside[:, at] = spread(steps, i, head_dim) * total + skips * d_own.astype(F32)


def input_kernel(b, incoming, inside, tail, grad, *, head_dim):
    width = inside.shape[1]
    tails = tail[...]
    for i in range(width // LANES):
        at = tile(LANES, i)
        right = dot(b[...], incoming[:, at], 1, 0)
        grad[:, at] = (inside[:, at] + spread(tails, i, head_dim) * right).astype(BF16)


def swap(value, axis):
    return lax.ppermute(value, axis, [(0, 1), (1, 0)])


def local(x, z, b, c, dt, decay, skip, gain, w_out, d_out, lengths):
    x, z, b, c, dt, decay, d_own = x[0], z[0], b[0], c[0], dt[0], decay[0], d_out[0]
    n, width = x.shape
    heads = dt.shape[1]
    head_dim = width // heads
    state_dim = b.shape[1]
    parts = lax.axis_size("seq")
    chans = lax.axis_size("chan")
    chan = lax.axis_index("chan")
    rows = state_dim // parts
    total = width * chans
    gain_row = gain[None, :]
    offset = (lax.axis_index("seq") * n).astype(jnp.int32)[None]

    if chans == 2:
        d_other = swap(d_own, "chan")
        first = chan == 0
        cotangent = jnp.concatenate(
            [jnp.where(first, d_own, d_other), jnp.where(first, d_other, d_own)], axis=1
        )
    else:
        cotangent = lax.all_gather(d_own, "chan", axis=1, tiled=True)

    payload, carry, tail = call(
        functools.partial(state_kernel, head_dim=head_dim),
        [((state_dim, width + LANES), BF16), ((n, heads), F32), ((n, heads), F32)],
        [VMEM] * 4 + [SMEM] * 2,
        [pltpu.VMEM((n, width), BF16)],
    )(x, b, dt, decay, lengths, offset)
    received = lax.all_to_all(
        payload.reshape(parts, rows, width + LANES), "seq", 0, 0, tiled=True
    )
    mixing, inside = call(
        functools.partial(mixing_kernel, head_dim=head_dim),
        [((heads, n, n), BF16), ((n, width), F32)],
        [VMEM] * 5 + [SMEM] * 2,
    )(x, b, c, dt, decay, lengths, offset)
    pulled = lax.dot_general(
        cotangent, w_out, (((1,), (1,)), ((), ())), preferred_element_type=F32
    )
    states, decays = call(
        functools.partial(onward_kernel, heads=heads, head_dim=head_dim),
        [((parts, rows, width), BF16), ((parts, width), F32)],
        [VMEM],
    )(received)
    incoming = lax.all_to_all(states, "seq", 0, 0, tiled=True).reshape(state_dim, width)
    gated, normed, stats = call(
        functools.partial(gated_kernel, head_dim=head_dim),
        [((n, width), F32), ((n, width), BF16), ((8, n), F32)],
        [VMEM] * 6 + [SMEM] + [VMEM] * 2,
    )(c, incoming, inside, carry, x, z, skip, gain_row, pulled)
    stats = stats + swap(stats, "chan") if chans == 2 else lax.psum(stats, "chan")
    d_ssd, payload, inverse = call(
        functools.partial(cotangent_kernel, head_dim=head_dim, total=total, rows=rows),
        [((n, width), BF16), ((state_dim, width + 2 * LANES), BF16), ((n, 1), F32)],
        [VMEM] * 8,
        [pltpu.VMEM((n, width), BF16), pltpu.VMEM((rows, 2 * LANES), F32)],
    )(stats, c, carry, x, z, gain_row, pulled, gated)
    received = lax.all_to_all(
        payload.reshape(parts, rows, width + 2 * LANES), "seq", 0, 0, tiled=True
    )
    grad_inside = call(
        functools.partial(inside_kernel, head_dim=head_dim),
        [((n, width), F32)],
        [VMEM] * 3 + [SMEM],
    )(mixing, d_ssd, dt, skip)[0]
    states, sums = call(
        backward_kernel,
        [((parts, rows, width), BF16), ((rows, 2 * LANES), F32)],
        [VMEM] * 2,
    )(received, decays)
    incoming = lax.all_to_all(states, "seq", 0, 0, tiled=True).reshape(state_dim, width)
    sums = sums + swap(sums, "dp") if lax.axis_size("dp") == 2 else lax.psum(sums, "dp")
    projected = jnp.dot(normed, w_out, preferred_element_type=F32)
    if chans == 2:
        half = projected.shape[1] // 2
        low, high = projected[:, :half], projected[:, half:]
        theirs = swap(jnp.where(chan == 0, high, low).astype(BF16), "chan")
        projected = jnp.where(chan == 0, low, high) + theirs.astype(F32)
    else:
        projected = lax.psum_scatter(
            projected.astype(BF16), "chan", scatter_dimension=1, tiled=True
        ).astype(F32)
    out = (inverse * projected).astype(BF16)[None]
    grad_x = call(
        functools.partial(input_kernel, head_dim=head_dim),
        [((n, width), BF16)],
        [VMEM] * 4,
    )(b, incoming, grad_inside, tail)[0][None]
    grad_gain = sums[:, :LANES].reshape(-1)
    grad_skip = jnp.sum(sums[:, LANES:].reshape(heads, head_dim), axis=1)
    return (out, grad_x, grad_gain, grad_skip)


def solution(mesh):
    return jax.shard_map(
        local,
        mesh=mesh,
        in_specs=(
            P("dp", "seq", "chan"),
            P("dp", "seq", "chan"),
            P("dp", "seq", None),
            P("dp", "seq", None),
            P("dp", "seq", "chan"),
            P("dp", "seq", "chan"),
            P("chan"),
            P("chan"),
            P("chan", None),
            P("dp", "seq", "chan"),
            P("dp", None),
        ),
        out_specs=(P("dp", "seq", "chan"), P("dp", "seq", "chan"), P("chan"), P("chan")),
        check_vma=False,
    )
```

time: 249 us -> 108 us (0.43)
  blocking collectives: 90.7 us -> 0 us
  waiting for transfers between devices: 69.7 us -> 34.6 us
  local copies, waits for them, and re-layouts: 33.3 us -> 6.8 us
  Pallas kernels: 0 us -> 25.6 us
  starting transfers between devices: 0.12 us -> 22.9 us
  between operations: 14.7 us -> 0.69 us
  matrix products: 25.7 us -> 12.1 us
  other arithmetic: 13.6 us -> 4.57 us
    all_gather x2 -> x0, waiting for transfers between devices: 69.6 us -> none  [the longest x1 40.1 us: local(): lax.all_gather(dev_state[None].astype(jnp.bfloat16), 'seq', axis=0, tiled...]
    all_gather x3 -> x0, blocking collectives: 47.8 us -> none  [the longest x1 22.6 us: local(): decays = lax.all_gather(dev_decay[None, :], 'seq', axis=0, tiled=True)]
    psum x3 -> x0, blocking collectives: 42.9 us -> none  [the longest x1 33.1 us: local(): grad_gain, grad_skip = lax.psum((gain_local, skip_local), ('seq', 'dp'))]
    all_to_all x0 -> x4, waiting for transfers between devices: none -> 30.1 us  [the longest x1 13.7 us: local(): lax.all_to_all(payload.reshape(parts, rows, width + LANES), 'seq', 0, 0,...]
    pallas_call x0 -> x8, Pallas kernels: none -> 25.6 us  [the longest x1 4.14 us: local(): call(functools.partial(gated_kernel, head_dim=head_dim), [((n, width), F3...]
    dynamic_slice x14 -> x0, local copies, waits for them, and re-layouts: 23.7 us -> none  [one(): lax.dynamic_index_in_dim(a, source, 0, False).astype(own.dtype)]
    all_to_all x0 -> x4, starting transfers between devices: none -> 18.2 us  [the longest x2 7.28 us: local(): lax.all_to_all(states, 'seq', 0, 0, tiled=True).reshape(state_dim, width)]
    dot_general x11 -> x2, matrix products: 25.7 us -> 12.1 us  [the longest x1 7.28 us: local(): lax.dot_general(cotangent, w_out, (((1,), (1,)), ((), ())), preferred_ele...]
  transfers between devices with their start and end apart: 3 -> 8, of which waited for: 2 -> 6; matrix products, arithmetic and copies ran while one was open for 6% -> 15% of each run, Pallas kernels for 0% -> 9%
where the time goes in v1:
time: 108 us; the launch traced here: 107 us
  waiting for transfers between devices  34.6 us (32%)
  Pallas kernels  25.6 us (24%)
  starting transfers between devices  22.9 us (21%)
  matrix products  12.1 us (11%)
  local copies, waits for them, and re-layouts  6.8 us (6%)
  other arithmetic  4.57 us (4%)
    all_to_all x1, waiting for transfers between devices, local(): lax.all_to_all(payload.reshape(parts, rows, width + LANES), 'seq', 0, 0,...  13.7 us
    all_to_all x1, waiting for transfers between devices, local(): lax.all_to_all(payload.reshape(parts, rows, width + 2 * LANES), 'seq', 0,...  10.1 us
    all_to_all x2, starting transfers between devices, local(): lax.all_to_all(states, 'seq', 0, 0, tiled=True).reshape(state_dim, width)  7.28 us
    all_to_all x1, starting transfers between devices, local(): lax.all_to_all(payload.reshape(parts, rows, width + LANES), 'seq', 0, 0,...  7.28 us
    dot_general x1, matrix products, local(): lax.dot_general(cotangent, w_out, (((1,), (1,)), ((), ())), preferred_ele...  7.28 us
    all_to_all x2, waiting for transfers between devices, local(): lax.all_to_all(states, 'seq', 0, 0, tiled=True).reshape(state_dim, width)  6.3 us
    unnamed x12, local copies, waits for them, and re-layouts  6.13 us
    dot_general x1, matrix products, local(): projected = jnp.dot(normed, w_out, preferred_element_type=F32)  4.84 us
  transfers between devices with their start and end apart: 8, of which 6 were waited for; matrix products, arithmetic and copies ran while one was open for 15% of the time, Pallas kernels for 9%

profile of v1, /device:TPU:0, one launch (start us, length us, event | category | flops | bytes accessed | tf_op | source)
XLA Modules:
  0.0 107.3 jit_solution(13639289992007351232)
XLA Ops:
  0.6 1.4 %copy.17 = f32[1,128,32]{2,1,0:T(8,128)} copy(f32[1,128,32]{1,2,0:T(8,128)} %param.15) | data formatting | bytes 32768 | tf_op args[4]
  2.1 1.4 %copy.18 = f32[1,128,32]{2,1,0:T(8,128)} copy(f32[1,128,32]{1,2,0:T(8,128)} %param.16) | data formatting | bytes 32768 | tf_op args[5]
  3.5 3.1 %state_kernel.1 = (bf16[128,2176]{1,0:T(8,128)(2,1)}, f32[128,32]{1,0:T(8,128)}, f32[128,32]{1,0:T(8,128)}) custom-call(bf16[128,2048]{1,0:T(8,128)(2,1)} %bitcast.23, bf16[128,128]{1,0:T(8,128)(2,1)} %bitcast.42, f32[128,32]{1,0:T(8,128)} %bitcast.31, f32[128,32]{1,0:T(8,128)} %bitcast.35, s32[1,4]{1,0:T(1,128)} %lengths.3, s32[1]{0:T(128)} %bitcast.5.offset), custom_call_target="tpu_custom_call" | custom-call | tf_op jit(solution)/shard_map/state_kernel/pallas_call | solution.py:255
  6.6 7.3 %all-to-all-start = ((bf16[8,16,2176]{2,1,0:T(8,128)(2,1)}), bf16[8,16,2176]{2,1,0:T(8,128)(2,1)S(1)}, u32[]{:S(2)}, u32[]{:S(2)}) async-start(bf16[8,16,2176]{2,1,0:T(8,128)(2,1)} %bitcast.37), calls=%async_computation | async-start | bytes 1114112 | tf_op jit(solution)/shard_map/all_to_all | solution.py:261
  13.9 1.5 %collective-permute-start = (bf16[128,1024]{1,0:T(8,128)(2,1)}, bf16[128,1024]{1,0:T(8,128)(2,1)S(1)}, u32[]{:S(2)}, u32[]{:S(2)}) collective-permute-start(bf16[128,1024]{1,0:T(8,128)(2,1)} %bitcast.45), channel_id=1, source_target_pairs={{0,2},{2,0},{1,3},{3,1},{4,6},{6,4},{5,7},{7,5},{8,10},{10,8},{9,1... | collective-permute-start | bytes 786440 | tf_op jit(solution)/shard_map/ppermute | solution.py:229
  15.4 13.7 %all-to-all-done.parts = bf16[8,16,2176]{2,1,0:T(8,128)(2,1)S(1)} async-done(((bf16[8,16,2176]{2,1,0:T(8,128)(2,1)}), bf16[8,16,2176]{2,1,0:T(8,128)(2,1)S(1)}, u32[]{:S(2)}, u32[]{:S(2)}) %all-to-all-start) | async-done | bytes 557088 | tf_op jit(solution)/shard_map/all_to_all | solution.py:261
  29.1 0.8 copy-done.1
  29.9 2.1 %onward_kernel.1 = (bf16[8,16,2048]{2,1,0:T(8,128)(2,1)}, f32[8,2048]{1,0:T(8,128)}) custom-call(bf16[8,16,2176]{2,1,0:T(8,128)(2,1)} %copy-done.1), custom_call_target="tpu_custom_call" | custom-call | tf_op jit(solution)/shard_map/onward_kernel/pallas_call | solution.py:272
  32.0 3.6 %all-to-all-start.1 = ((bf16[8,16,2048]{2,1,0:T(8,128)(2,1)}), bf16[8,16,2048]{2,1,0:T(8,128)(2,1)S(1)}, u32[]{:S(2)}, u32[]{:S(2)}) async-start(bf16[8,16,2048]{2,1,0:T(8,128)(2,1)} %get-tuple-element.20), calls=%async_computation.1 | async-start | bytes 1048576 | tf_op jit(solution)/shard_map/all_to_all | solution.py:277
  35.7 3.9 %mixing_kernel.1 = (bf16[32,128,128]{2,1,0:T(8,128)(2,1)}, f32[128,2048]{1,0:T(8,128)}) custom-call(bf16[128,2048]{1,0:T(8,128)(2,1)} %bitcast.24, bf16[128,128]{1,0:T(8,128)(2,1)} %bitcast.43, bf16[128,128]{1,0:T(8,128)(2,1)} %bitcast.39, f32[128,32]{1,0:T(8,128)} %bitcast.32, f32[128,32]{1,0:T(8,128)} %bitcast.36, s32[1,4]{1,0:T(1,128)} %lengths.3, ...), custom_call_target="tpu_custom_call" | custom-call | tf_op jit(solution)/shard_map/mixing_kernel/pallas_call | solution.py:264
  39.6 1.0 broadcast_select_fusion.1
  40.6 7.3 %fusion.pulled = f32[128,2048]{1,0:T(8,128)} fusion(bf16[2048,2048]{1,0:T(8,128)(2,1)} %param.19, bf16[128,1024]{1,0:T(8,128)(2,1)S(1)} %get-tuple-element.35, bf16[128,1024]{1,0:T(8,128)(2,1)S(1)} %get-tuple-element.34), kind=kOutput, calls=%fused_computation | convolution fusion | flops 1074790400 | bytes 9961472 | tf_op jit(solution)/shard_map/dot_general | solution.py:269
  47.8 2.5 %all-to-all-done.1 = bf16[8,16,2048]{2,1,0:T(8,128)(2,1)S(1)} async-done(((bf16[8,16,2048]{2,1,0:T(8,128)(2,1)}), bf16[8,16,2048]{2,1,0:T(8,128)(2,1)S(1)}, u32[]{:S(2)}, u32[]{:S(2)}) %all-to-all-start.1) | async-done | bytes 524320 | tf_op jit(solution)/shard_map/all_to_all | solution.py:277
  50.3 0.8 copy-done.3
  51.1 4.1 %gated_kernel.1 = (f32[128,2048]{1,0:T(8,128)}, bf16[128,2048]{1,0:T(8,128)(2,1)}, f32[8,128]{1,0:T(8,128)}) custom-call(bf16[128,128]{1,0:T(8,128)(2,1)} %bitcast.40, bf16[128,2048]{1,0:T(8,128)(2,1)} %bitcast.30, f32[128,2048]{1,0:T(8,128)} %get-tuple-element.21.inside, f32[128,32]{1,0:T(8,128)} %get-tuple-element.22.carry, bf16[128,2048]{1,0:T(8,128)(2,1)} %bitcast.25, ...), custom_call_target="tpu_custom_call" | custom-call | tf_op jit(solution)/shard_map/gated_kernel/pallas_call | solution.py:278
  55.3 1.5 %collective-permute-start.1 = (f32[8,128]{1,0:T(8,128)}, f32[8,128]{1,0:T(8,128)S(1)}, u32[]{:S(2)}, u32[]{:S(2)}) collective-permute-start(f32[8,128]{1,0:T(8,128)} %get-tuple-element.23), channel_id=1, source_target_pairs={{0,2},{2,0},{1,3},{3,1},{4,6},{6,4},{5,7},{7,5},{8,10},{10,8},{9,1... | collective-permute-start | bytes 12296 | tf_op jit(solution)/shard_map/ppermute | solution.py:229
  56.8 2.3 %collective-permute-done.1 = f32[8,128]{1,0:T(8,128)S(1)} collective-permute-done((f32[8,128]{1,0:T(8,128)}, f32[8,128]{1,0:T(8,128)S(1)}, u32[]{:S(2)}, u32[]{:S(2)}) %collective-permute-start.1) | collective-permute-done | bytes 4128 | tf_op jit(solution)/shard_map/ppermute | solution.py:229
  59.1 1.3 %add.9.stats = f32[8,128]{1,0:T(8,128)} add(f32[8,128]{1,0:T(8,128)} %get-tuple-element.23, f32[8,128]{1,0:T(8,128)S(1)} %collective-permute-done.1) | non-fusion elementwise | flops 1024 | bytes 12288 | tf_op jit(solution)/shard_map/add | solution.py:283
  60.4 4.1 %cotangent_kernel.1 = (bf16[128,2048]{1,0:T(8,128)(2,1)}, bf16[128,2304]{1,0:T(8,128)(2,1)}, f32[128,1]{1,0:T(8,128)}) custom-call(f32[8,128]{1,0:T(8,128)} %add.9.stats, bf16[128,128]{1,0:T(8,128)(2,1)} %bitcast.41, f32[128,32]{1,0:T(8,128)} %get-tuple-element.22.carry, bf16[128,2048]{1,0:T(8,128)(2,1)} %bitcast.26, bf16[128,2048]{1,0:T(8,128)(2,1)} %bitcast.28, ...), custom_call_target="tpu_custom_call" | custom-call | tf_op jit(solution)/shard_map/cotangent_kernel/pallas_call | solution.py:284
  64.4 3.6 %all-to-all-start.2 = ((bf16[8,16,2304]{2,1,0:T(8,128)(2,1)}), bf16[8,16,2304]{2,1,0:T(8,128)(2,1)S(1)}, u32[]{:S(2)}, u32[]{:S(2)}) async-start(bf16[8,16,2304]{2,1,0:T(8,128)(2,1)} %bitcast.34), calls=%async_computation.2 | async-start | bytes 1179648 | tf_op jit(solution)/shard_map/all_to_all | solution.py:290
  68.1 4.8 %fusion.7 = f32[128,2048]{1,0:T(8,128)S(1)} fusion(bf16[128,2048]{1,0:T(8,128)(2,1)} %get-tuple-element.26, bf16[2048,2048]{1,0:T(8,128)(2,1)} %param.19), kind=kOutput, calls=%fused_computation.12 | convolution fusion | flops 1073741824 | bytes 9961472 | tf_op jit(solution)/shard_map/dot_general | solution.py:305
  72.9 10.1 %all-to-all-done.2.parts = bf16[8,16,2304]{2,1,0:T(8,128)(2,1)S(1)} async-done(((bf16[8,16,2304]{2,1,0:T(8,128)(2,1)}), bf16[8,16,2304]{2,1,0:T(8,128)(2,1)S(1)}, u32[]{:S(2)}, u32[]{:S(2)}) %all-to-all-start.2) | async-done | bytes 589856 | tf_op jit(solution)/shard_map/all_to_all | solution.py:290
  83.0 0.8 copy-done
  83.9 2.0 %backward_kernel.1 = (bf16[8,16,2048]{2,1,0:T(8,128)(2,1)}, f32[16,256]{1,0:T(8,128)}) custom-call(bf16[8,16,2304]{2,1,0:T(8,128)(2,1)} %copy-done, f32[8,2048]{1,0:T(8,128)} %get-tuple-element.28.decays), custom_call_target="tpu_custom_call" | custom-call | tf_op jit(solution)/shard_map/backward_kernel/pallas_call | solution.py:298
  85.9 3.6 %all-to-all-start.3 = ((bf16[8,16,2048]{2,1,0:T(8,128)(2,1)}), bf16[8,16,2048]{2,1,0:T(8,128)(2,1)S(1)}, u32[]{:S(2)}, u32[]{:S(2)}) async-start(bf16[8,16,2048]{2,1,0:T(8,128)(2,1)} %get-tuple-element.29), calls=%async_computation.3 | async-start | bytes 1048576 | tf_op jit(solution)/shard_map/all_to_all | solution.py:303
  89.6 1.6 %collective-permute-start.2 = (bf16[128,1024]{1,0:T(8,128)(2,1)S(1)}, bf16[128,1024]{1,0:T(8,128)(2,1)S(1)}, u32[]{:S(2)}, u32[]{:S(2)}) collective-permute-start(bf16[128,1024]{1,0:T(8,128)(2,1)S(1)} %select_convert_fusion), channel_id=1, source_target_pairs={{0,2},{2,0},{1,3},{3,1},{4,6},{6,4},{5,7},{7,5},{8,10},{10,8},{9,1... | collective-permute-start | bytes 786440 | tf_op jit(solution)/shard_map/ppermute | solution.py:229
  91.1 3.3 %inside_kernel.1.inside = f32[128,2048]{1,0:T(8,128)} custom-call(bf16[32,128,128]{2,1,0:T(8,128)(2,1)} %get-tuple-element.30.mixing, bf16[128,2048]{1,0:T(8,128)(2,1)} %get-tuple-element.31.d_ssd, f32[128,32]{1,0:T(8,128)} %bitcast.33, f32[32]{0:T(128)} %skip.3), custom_call_target="tpu_custom_call" | custom-call | tf_op jit(solution)/shard_map/inside_kernel/pallas_call | solution.py:293
  94.7 2.2 %collective-permute-done.2 = bf16[128,1024]{1,0:T(8,128)(2,1)S(1)} collective-permute-done((bf16[128,1024]{1,0:T(8,128)(2,1)S(1)}, bf16[128,1024]{1,0:T(8,128)(2,1)S(1)}, u32[]{:S(2)}, u32[]{:S(2)}) %collective-permute-start.2) | collective-permute-done | bytes 262176 | tf_op jit(solution)/shard_map/ppermute | solution.py:229
  96.9 0.8 fusion.4
  99.7 3.8 %all-to-all-done.3 = bf16[8,16,2048]{2,1,0:T(8,128)(2,1)S(1)} async-done(((bf16[8,16,2048]{2,1,0:T(8,128)(2,1)}), bf16[8,16,2048]{2,1,0:T(8,128)(2,1)S(1)}, u32[]{:S(2)}, u32[]{:S(2)}) %all-to-all-start.3) | async-done | bytes 524320 | tf_op jit(solution)/shard_map/all_to_all | solution.py:303
  103.6 0.8 copy-done.2
  104.4 2.9 %input_kernel.1 = bf16[128,2048]{1,0:T(8,128)(2,1)} custom-call(bf16[128,128]{1,0:T(8,128)(2,1)} %bitcast.44, bf16[128,2048]{1,0:T(8,128)(2,1)} %bitcast.29, f32[128,2048]{1,0:T(8,128)} %inside_kernel.1.inside, f32[128,32]{1,0:T(8,128)} %get-tuple-element.32.tail), custom_call_target="tpu_custom_call" | custom-call | tf_op jit(solution)/shard_map/input_kernel/pallas_call | solution.py:316
  (15 shorter events, 2.3 us)
Async XLA Ops:
  6.6 22.5 %all-to-all-start = ((bf16[8,16,2176]{2,1,0:T(8,128)(2,1)}), bf16[8,16,2176]{2,1,0:T(8,128)(2,1)S(1)}, u32[]{:S(2)}, u32[]{:S(2)}) async-start(bf16[8,16,2176]{2,1,0:T(8,128)(2,1)} %bitcast.37), calls=%async_computation | async-start | bytes 1114112 | tf_op jit(solution)/shard_map/all_to_all | solution.py:261
  13.9 25.7 %collective-permute-start = (bf16[128,1024]{1,0:T(8,128)(2,1)}, bf16[128,1024]{1,0:T(8,128)(2,1)S(1)}, u32[]{:S(2)}, u32[]{:S(2)}) collective-permute-start(bf16[128,1024]{1,0:T(8,128)(2,1)} %bitcast.45), channel_id=1, source_target_pairs={{0,2},{2,0},{1,3},{3,1},{4,6},{6,4},{5,7},{7,5},{8,10},{10,8},{9,1... | collective-permute-start | bytes 786440 | tf_op jit(solution)/shard_map/ppermute | solution.py:229
  29.1 0.8 copy-start.1
  32.0 18.3 %all-to-all-start.1 = ((bf16[8,16,2048]{2,1,0:T(8,128)(2,1)}), bf16[8,16,2048]{2,1,0:T(8,128)(2,1)S(1)}, u32[]{:S(2)}, u32[]{:S(2)}) async-start(bf16[8,16,2048]{2,1,0:T(8,128)(2,1)} %get-tuple-element.20), calls=%async_computation.1 | async-start | bytes 1048576 | tf_op jit(solution)/shard_map/all_to_all | solution.py:277
  50.3 0.8 copy-start.3
  55.3 3.8 %collective-permute-start.1 = (f32[8,128]{1,0:T(8,128)}, f32[8,128]{1,0:T(8,128)S(1)}, u32[]{:S(2)}, u32[]{:S(2)}) collective-permute-start(f32[8,128]{1,0:T(8,128)} %get-tuple-element.23), channel_id=1, source_target_pairs={{0,2},{2,0},{1,3},{3,1},{4,6},{6,4},{5,7},{7,5},{8,10},{10,8},{9,1... | collective-permute-start | bytes 12296 | tf_op jit(solution)/shard_map/ppermute | solution.py:229
  64.4 18.6 %all-to-all-start.2 = ((bf16[8,16,2304]{2,1,0:T(8,128)(2,1)}), bf16[8,16,2304]{2,1,0:T(8,128)(2,1)S(1)}, u32[]{:S(2)}, u32[]{:S(2)}) async-start(bf16[8,16,2304]{2,1,0:T(8,128)(2,1)} %bitcast.34), calls=%async_computation.2 | async-start | bytes 1179648 | tf_op jit(solution)/shard_map/all_to_all | solution.py:290
  68.1 26.4 %copy-start.4 = (f32[128,1]{1,0:T(8,128)S(1)}, f32[128,1]{1,0:T(8,128)}, u32[]{:S(2)}) copy-start(f32[128,1]{1,0:T(8,128)} %get-tuple-element.25) | copy-start | bytes 1540
  83.0 0.8 copy-start
  85.9 17.7 %all-to-all-start.3 = ((bf16[8,16,2048]{2,1,0:T(8,128)(2,1)}), bf16[8,16,2048]{2,1,0:T(8,128)(2,1)S(1)}, u32[]{:S(2)}, u32[]{:S(2)}) async-start(bf16[8,16,2048]{2,1,0:T(8,128)(2,1)} %get-tuple-element.29), calls=%async_computation.3 | async-start | bytes 1048576 | tf_op jit(solution)/shard_map/all_to_all | solution.py:303
  89.6 7.4 %collective-permute-start.2 = (bf16[128,1024]{1,0:T(8,128)(2,1)S(1)}, bf16[128,1024]{1,0:T(8,128)(2,1)S(1)}, u32[]{:S(2)}, u32[]{:S(2)}) collective-permute-start(bf16[128,1024]{1,0:T(8,128)(2,1)S(1)} %select_convert_fusion), channel_id=1, source_target_pairs={{0,2},{2,0},{1,3},{3,1},{4,6},{6,4},{5,7},{7,5},{8,10},{10,8},{9,1... | collective-permute-start | bytes 786440 | tf_op jit(solution)/shard_map/ppermute | solution.py:229
  94.6 3.1 %collective-permute-start.3 = (f32[16,256]{1,0:T(8,128)}, f32[16,256]{1,0:T(8,128)S(1)}, u32[]{:S(2)}, u32[]{:S(2)}) collective-permute-start(f32[16,256]{1,0:T(8,128)} %get-tuple-element.33), channel_id=1, source_target_pairs={{0,1},{1,0},{2,3},{3,2},{4,5},{5,4},{6,7},{7,6},{8,9},{9,8},{10,11... | collective-permute-start | bytes 49160 | tf_op jit(solution)/shard_map/ppermute | solution.py:229
  103.6 0.8 copy-start.2

commit v2 on v1

--- a/solution.py
+++ b/solution.py
@@ -58,6 +58,11 @@
     return total
 
 
+def turned(rows):
+    heads, n = rows.shape
+    return jnp.concatenate([rows] * (n // heads), axis=0).T[:, :heads]
+
+
 def triangle(n, upper):
     row = lax.broadcasted_iota(jnp.int32, (n, n), 0)
     col = lax.broadcasted_iota(jnp.int32, (n, n), 1)
@@ -65,15 +70,15 @@
 
 
 def state_kernel(x, b, dt, decay, lengths, offset, payload, carry, tail, scaled, *, head_dim):
-    n, heads = dt.shape
+    heads, n = dt.shape
     width = x.shape[1]
-    running = dot(triangle(n, False), decay[...], 1, 0, PRECISE)
+    running = dot(triangle(n, False), decay[...], 1, 1, PRECISE)
     position = lax.broadcasted_iota(jnp.int32, (n, 1), 0)
     count = counts(lengths, offset[0], position)
     end = counts(lengths, offset[0], jnp.full((1, 1), n - 1, jnp.int32))
     last = running[n - 1 : n, :]
     carry[...] = jnp.where(count == 0, jnp.exp(running), 0.0)
-    tails = jnp.where(count == end, jnp.exp(last - running), 0.0) * dt[...]
+    tails = jnp.where(count == end, jnp.exp(last - running), 0.0) * turned(dt[...])
     tail[...] = tails
     for i in range(width // LANES):
         at = tile(LANES, i)
@@ -90,17 +95,17 @@
 
 
 def mixing_kernel(x, b, c, dt, decay, lengths, offset, mixing, inside, *, head_dim):
-    n, heads = dt.shape
+    heads, n = dt.shape
     width = x.shape[1]
     per = LANES // head_dim
-    running = dot(triangle(n, False), decay[...], 1, 0, PRECISE)
-    across = dot(decay[...], triangle(n, True), 0, 0, PRECISE)
+    running = dot(triangle(n, False), decay[...], 1, 1, PRECISE)
+    across = dot(decay[...], triangle(n, True), 1, 0, PRECISE)
     t = lax.broadcasted_iota(jnp.int32, (n, n), 0)
     s = lax.broadcasted_iota(jnp.int32, (n, n), 1)
     same = counts(lengths, offset[0], t) == counts(lengths, offset[0], s)
     scores = jnp.where((t >= s) & same, dot(c[...], b[...], 1, 1), 0.0)
     lane = lax.broadcasted_iota(jnp.int32, (n, LANES), 1) // head_dim
-    steps = dt[...]
+    steps = turned(dt[...])
     for i in range(width // LANES):
         at = tile(LANES, i)
         stepped = spread(steps, i, head_dim) * x[:, at].astype(F32)
@@ -203,7 +208,7 @@
 def inside_kernel(mixing, d_ssd, dt, skip, inside, *, head_dim):
     n, width = d_ssd.shape
     per = LANES // head_dim
-    steps = dt[...]
+    steps = turned(dt[...])
     lane = lax.broadcasted_iota(jnp.int32, (n, LANES), 1)
     for i in range(width // LANES):
         at = tile(LANES, i)
@@ -232,7 +237,8 @@
 def local(x, z, b, c, dt, decay, skip, gain, w_out, d_out, lengths):
     x, z, b, c, dt, decay, d_own = x[0], z[0], b[0], c[0], dt[0], decay[0], d_out[0]
     n, width = x.shape
-    heads = dt.shape[1]
+    dt, decay = dt.T, decay.T
+    heads = dt.shape[0]
     head_dim = width // heads
     state_dim = b.shape[1]
     parts = lax.axis_size("seq")

time: 108 us -> 105 us (0.972)
  local copies, waits for them, and re-layouts: 6.8 us -> 3.92 us
    unnamed x12 -> x10, local copies, waits for them, and re-layouts: 6.13 us -> 3.25 us
where the time goes in v2:
time: 105 us; the launch traced here: 104 us
  waiting for transfers between devices  34.6 us (33%)
  Pallas kernels  25.7 us (24%)
  starting transfers between devices  22.9 us (22%)
  matrix products  12.1 us (12%)
  other arithmetic  4.57 us (4%)
  local copies, waits for them, and re-layouts  3.92 us (4%)
    all_to_all x1, waiting for transfers between devices, local(): lax.all_to_all(payload.reshape(parts, rows, width + LANES), 'seq', 0, 0,...  13.7 us
    all_to_all x1, waiting for transfers between devices, local(): lax.all_to_all(payload.reshape(parts, rows, width + 2 * LANES), 'seq', 0,...  10.1 us
    all_to_all x1, starting transfers between devices, local(): lax.all_to_all(payload.reshape(parts, rows, width + LANES), 'seq', 0, 0,...  7.28 us
    all_to_all x2, starting transfers between devices, local(): lax.all_to_all(states, 'seq', 0, 0, tiled=True).reshape(state_dim, width)  7.28 us
    dot_general x1, matrix products, local(): lax.dot_general(cotangent, w_out, (((1,), (1,)), ((), ())), preferred_ele...  7.28 us
    all_to_all x2, waiting for transfers between devices, local(): lax.all_to_all(states, 'seq', 0, 0, tiled=True).reshape(state_dim, width)  6.3 us
    dot_general x1, matrix products, local(): projected = jnp.dot(normed, w_out, preferred_element_type=F32)  4.84 us
    ppermute x4, starting transfers between devices, swap(): return lax.ppermute(value, axis, [(0, 1), (1, 0)])  4.69 us
  transfers between devices with their start and end apart: 8, of which 6 were waited for; matrix products, arithmetic and copies ran while one was open for 15% of the time, Pallas kernels for 9%

profile of v2, /device:TPU:0, one launch (start us, length us, event | category | flops | bytes accessed | tf_op | source)
XLA Modules:
  0.0 104.5 jit_solution(12933157992562578997)
XLA Ops:
  0.6 3.2 %state_kernel.1 = (bf16[128,2176]{1,0:T(8,128)(2,1)}, f32[128,32]{1,0:T(8,128)}, f32[128,32]{1,0:T(8,128)}) custom-call(bf16[128,2048]{1,0:T(8,128)(2,1)} %bitcast.27, bf16[128,128]{1,0:T(8,128)(2,1)} %bitcast.41, f32[32,128]{1,0:T(8,128)} %bitcast.45, f32[32,128]{1,0:T(8,128)} %bitcast.48, s32[1,4]{1,0:T(1,128)} %lengths.3, s32[1]{0:T(128)} %bitcast.7.offset), custom_call_target="tpu_custom_call" | custom-call | tf_op jit(solution)/shard_map/state_kernel/pallas_call | solution.py:261
  3.8 7.3 %all-to-all-start = ((bf16[8,16,2176]{2,1,0:T(8,128)(2,1)}), bf16[8,16,2176]{2,1,0:T(8,128)(2,1)S(1)}, u32[]{:S(2)}, u32[]{:S(2)}) async-start(bf16[8,16,2176]{2,1,0:T(8,128)(2,1)} %bitcast.36), calls=%async_computation | async-start | bytes 1114112 | tf_op jit(solution)/shard_map/all_to_all | solution.py:267
  11.1 1.5 %collective-permute-start = (bf16[128,1024]{1,0:T(8,128)(2,1)}, bf16[128,1024]{1,0:T(8,128)(2,1)S(1)}, u32[]{:S(2)}, u32[]{:S(2)}) collective-permute-start(bf16[128,1024]{1,0:T(8,128)(2,1)} %bitcast.44), channel_id=1, source_target_pairs={{0,2},{2,0},{1,3},{3,1},{4,6},{6,4},{5,7},{7,5},{8,10},{10,8},{9,1... | collective-permute-start | bytes 786440 | tf_op jit(solution)/shard_map/ppermute | solution.py:234
  12.6 13.7 %all-to-all-done.parts = bf16[8,16,2176]{2,1,0:T(8,128)(2,1)S(1)} async-done(((bf16[8,16,2176]{2,1,0:T(8,128)(2,1)}), bf16[8,16,2176]{2,1,0:T(8,128)(2,1)S(1)}, u32[]{:S(2)}, u32[]{:S(2)}) %all-to-all-start) | async-done | bytes 557088 | tf_op jit(solution)/shard_map/all_to_all | solution.py:267
  26.3 0.8 copy-done.1
  27.1 2.1 %onward_kernel.1 = (bf16[8,16,2048]{2,1,0:T(8,128)(2,1)}, f32[8,2048]{1,0:T(8,128)}) custom-call(bf16[8,16,2176]{2,1,0:T(8,128)(2,1)} %copy-done.1), custom_call_target="tpu_custom_call" | custom-call | tf_op jit(solution)/shard_map/onward_kernel/pallas_call | solution.py:278
  29.2 3.6 %all-to-all-start.1 = ((bf16[8,16,2048]{2,1,0:T(8,128)(2,1)}), bf16[8,16,2048]{2,1,0:T(8,128)(2,1)S(1)}, u32[]{:S(2)}, u32[]{:S(2)}) async-start(bf16[8,16,2048]{2,1,0:T(8,128)(2,1)} %get-tuple-element.20), calls=%async_computation.1 | async-start | bytes 1048576 | tf_op jit(solution)/shard_map/all_to_all | solution.py:283
  32.9 3.9 %mixing_kernel.1 = (bf16[32,128,128]{2,1,0:T(8,128)(2,1)}, f32[128,2048]{1,0:T(8,128)}) custom-call(bf16[128,2048]{1,0:T(8,128)(2,1)} %bitcast.28, bf16[128,128]{1,0:T(8,128)(2,1)} %bitcast.42, bf16[128,128]{1,0:T(8,128)(2,1)} %bitcast.38, f32[32,128]{1,0:T(8,128)} %bitcast.46, f32[32,128]{1,0:T(8,128)} %bitcast.49, s32[1,4]{1,0:T(1,128)} %lengths.3, ...), custom_call_target="tpu_custom_call" | custom-call | tf_op jit(solution)/shard_map/mixing_kernel/pallas_call | solution.py:270
  36.8 1.0 broadcast_select_fusion.1
  37.8 7.3 %fusion.pulled = f32[128,2048]{1,0:T(8,128)} fusion(bf16[2048,2048]{1,0:T(8,128)(2,1)} %param.19, bf16[128,1024]{1,0:T(8,128)(2,1)S(1)} %get-tuple-element.35, bf16[128,1024]{1,0:T(8,128)(2,1)S(1)} %get-tuple-element.34), kind=kOutput, calls=%fused_computation | convolution fusion | flops 1074790400 | bytes 9961472 | tf_op jit(solution)/shard_map/dot_general | solution.py:275
  45.1 2.5 %all-to-all-done.1 = bf16[8,16,2048]{2,1,0:T(8,128)(2,1)S(1)} async-done(((bf16[8,16,2048]{2,1,0:T(8,128)(2,1)}), bf16[8,16,2048]{2,1,0:T(8,128)(2,1)S(1)}, u32[]{:S(2)}, u32[]{:S(2)}) %all-to-all-start.1) | async-done | bytes 524320 | tf_op jit(solution)/shard_map/all_to_all | solution.py:283
  47.5 0.8 copy-done.3
  48.3 4.1 %gated_kernel.1 = (f32[128,2048]{1,0:T(8,128)}, bf16[128,2048]{1,0:T(8,128)(2,1)}, f32[8,128]{1,0:T(8,128)}) custom-call(bf16[128,128]{1,0:T(8,128)(2,1)} %bitcast.39, bf16[128,2048]{1,0:T(8,128)(2,1)} %bitcast.34, f32[128,2048]{1,0:T(8,128)} %get-tuple-element.21.inside, f32[128,32]{1,0:T(8,128)} %get-tuple-element.22.carry, bf16[128,2048]{1,0:T(8,128)(2,1)} %bitcast.29, ...), custom_call_target="tpu_custom_call" | custom-call | tf_op jit(solution)/shard_map/gated_kernel/pallas_call | solution.py:284
  52.5 1.5 %collective-permute-start.1 = (f32[8,128]{1,0:T(8,128)}, f32[8,128]{1,0:T(8,128)S(1)}, u32[]{:S(2)}, u32[]{:S(2)}) collective-permute-start(f32[8,128]{1,0:T(8,128)} %get-tuple-element.23), channel_id=1, source_target_pairs={{0,2},{2,0},{1,3},{3,1},{4,6},{6,4},{5,7},{7,5},{8,10},{10,8},{9,1... | collective-permute-start | bytes 12296 | tf_op jit(solution)/shard_map/ppermute | solution.py:234
  54.0 2.3 %collective-permute-done.1 = f32[8,128]{1,0:T(8,128)S(1)} collective-permute-done((f32[8,128]{1,0:T(8,128)}, f32[8,128]{1,0:T(8,128)S(1)}, u32[]{:S(2)}, u32[]{:S(2)}) %collective-permute-start.1) | collective-permute-done | bytes 4128 | tf_op jit(solution)/shard_map/ppermute | solution.py:234
  56.3 1.3 %add.9.stats = f32[8,128]{1,0:T(8,128)} add(f32[8,128]{1,0:T(8,128)} %get-tuple-element.23, f32[8,128]{1,0:T(8,128)S(1)} %collective-permute-done.1) | non-fusion elementwise | flops 1024 | bytes 12288 | tf_op jit(solution)/shard_map/add | solution.py:289
  57.6 4.1 %cotangent_kernel.1 = (bf16[128,2048]{1,0:T(8,128)(2,1)}, bf16[128,2304]{1,0:T(8,128)(2,1)}, f32[128,1]{1,0:T(8,128)}) custom-call(f32[8,128]{1,0:T(8,128)} %add.9.stats, bf16[128,128]{1,0:T(8,128)(2,1)} %bitcast.40, f32[128,32]{1,0:T(8,128)} %get-tuple-element.22.carry, bf16[128,2048]{1,0:T(8,128)(2,1)} %bitcast.30, bf16[128,2048]{1,0:T(8,128)(2,1)} %bitcast.32, ...), custom_call_target="tpu_custom_call" | custom-call | tf_op jit(solution)/shard_map/cotangent_kernel/pallas_call | solution.py:290
  61.6 3.6 %all-to-all-start.2 = ((bf16[8,16,2304]{2,1,0:T(8,128)(2,1)}), bf16[8,16,2304]{2,1,0:T(8,128)(2,1)S(1)}, u32[]{:S(2)}, u32[]{:S(2)}) async-start(bf16[8,16,2304]{2,1,0:T(8,128)(2,1)} %bitcast.35), calls=%async_computation.2 | async-start | bytes 1179648 | tf_op jit(solution)/shard_map/all_to_all | solution.py:296
  65.3 4.8 %fusion.7 = f32[128,2048]{1,0:T(8,128)S(1)} fusion(bf16[128,2048]{1,0:T(8,128)(2,1)} %get-tuple-element.26, bf16[2048,2048]{1,0:T(8,128)(2,1)} %param.19), kind=kOutput, calls=%fused_computation.12 | convolution fusion | flops 1073741824 | bytes 9961472 | tf_op jit(solution)/shard_map/dot_general | solution.py:311
  70.1 10.1 %all-to-all-done.2.parts = bf16[8,16,2304]{2,1,0:T(8,128)(2,1)S(1)} async-done(((bf16[8,16,2304]{2,1,0:T(8,128)(2,1)}), bf16[8,16,2304]{2,1,0:T(8,128)(2,1)S(1)}, u32[]{:S(2)}, u32[]{:S(2)}) %all-to-all-start.2) | async-done | bytes 589856 | tf_op jit(solution)/shard_map/all_to_all | solution.py:296
  80.2 0.8 copy-done
  81.1 2.0 %backward_kernel.1 = (bf16[8,16,2048]{2,1,0:T(8,128)(2,1)}, f32[16,256]{1,0:T(8,128)}) custom-call(bf16[8,16,2304]{2,1,0:T(8,128)(2,1)} %copy-done, f32[8,2048]{1,0:T(8,128)} %get-tuple-element.28.decays), custom_call_target="tpu_custom_call" | custom-call | tf_op jit(solution)/shard_map/backward_kernel/pallas_call | solution.py:304
  83.1 3.6 %all-to-all-start.3 = ((bf16[8,16,2048]{2,1,0:T(8,128)(2,1)}), bf16[8,16,2048]{2,1,0:T(8,128)(2,1)S(1)}, u32[]{:S(2)}, u32[]{:S(2)}) async-start(bf16[8,16,2048]{2,1,0:T(8,128)(2,1)} %get-tuple-element.29), calls=%async_computation.3 | async-start | bytes 1048576 | tf_op jit(solution)/shard_map/all_to_all | solution.py:309
  86.8 1.6 %collective-permute-start.2 = (bf16[128,1024]{1,0:T(8,128)(2,1)S(1)}, bf16[128,1024]{1,0:T(8,128)(2,1)S(1)}, u32[]{:S(2)}, u32[]{:S(2)}) collective-permute-start(bf16[128,1024]{1,0:T(8,128)(2,1)S(1)} %select_convert_fusion), channel_id=1, source_target_pairs={{0,2},{2,0},{1,3},{3,1},{4,6},{6,4},{5,7},{7,5},{8,10},{10,8},{9,1... | collective-permute-start | bytes 786440 | tf_op jit(solution)/shard_map/ppermute | solution.py:234
  88.4 3.3 %inside_kernel.1.inside = f32[128,2048]{1,0:T(8,128)} custom-call(bf16[32,128,128]{2,1,0:T(8,128)(2,1)} %get-tuple-element.30.mixing, bf16[128,2048]{1,0:T(8,128)(2,1)} %get-tuple-element.31.d_ssd, f32[32,128]{1,0:T(8,128)} %bitcast.47, f32[32]{0:T(128)} %skip.3), custom_call_target="tpu_custom_call" | custom-call | tf_op jit(solution)/shard_map/inside_kernel/pallas_call | solution.py:299
  91.9 2.2 %collective-permute-done.2 = bf16[128,1024]{1,0:T(8,128)(2,1)S(1)} collective-permute-done((bf16[128,1024]{1,0:T(8,128)(2,1)S(1)}, bf16[128,1024]{1,0:T(8,128)(2,1)S(1)}, u32[]{:S(2)}, u32[]{:S(2)}) %collective-permute-start.2) | collective-permute-done | bytes 262176 | tf_op jit(solution)/shard_map/ppermute | solution.py:234
  94.1 0.8 fusion.4
  94.9 0.7 add.11
  96.3 0.6 reduce_sum.9
  97.0 3.8 %all-to-all-done.3 = bf16[8,16,2048]{2,1,0:T(8,128)(2,1)S(1)} async-done(((bf16[8,16,2048]{2,1,0:T(8,128)(2,1)}), bf16[8,16,2048]{2,1,0:T(8,128)(2,1)S(1)}, u32[]{:S(2)}, u32[]{:S(2)}) %all-to-all-start.3) | async-done | bytes 524320 | tf_op jit(solution)/shard_map/all_to_all | solution.py:309
  100.8 0.8 copy-done.2
  101.6 2.9 %input_kernel.1 = bf16[128,2048]{1,0:T(8,128)(2,1)} custom-call(bf16[128,128]{1,0:T(8,128)(2,1)} %bitcast.43, bf16[128,2048]{1,0:T(8,128)(2,1)} %bitcast.33, f32[128,2048]{1,0:T(8,128)} %inside_kernel.1.inside, f32[128,32]{1,0:T(8,128)} %get-tuple-element.32.tail), custom_call_target="tpu_custom_call" | custom-call | tf_op jit(solution)/shard_map/input_kernel/pallas_call | solution.py:322
  (13 shorter events, 0.9 us)
Async XLA Ops:
  3.8 22.5 %all-to-all-start = ((bf16[8,16,2176]{2,1,0:T(8,128)(2,1)}), bf16[8,16,2176]{2,1,0:T(8,128)(2,1)S(1)}, u32[]{:S(2)}, u32[]{:S(2)}) async-start(bf16[8,16,2176]{2,1,0:T(8,128)(2,1)} %bitcast.36), calls=%async_computation | async-start | bytes 1114112 | tf_op jit(solution)/shard_map/all_to_all | solution.py:267
  11.1 25.7 %collective-permute-start = (bf16[128,1024]{1,0:T(8,128)(2,1)}, bf16[128,1024]{1,0:T(8,128)(2,1)S(1)}, u32[]{:S(2)}, u32[]{:S(2)}) collective-permute-start(bf16[128,1024]{1,0:T(8,128)(2,1)} %bitcast.44), channel_id=1, source_target_pairs={{0,2},{2,0},{1,3},{3,1},{4,6},{6,4},{5,7},{7,5},{8,10},{10,8},{9,1... | collective-permute-start | bytes 786440 | tf_op jit(solution)/shard_map/ppermute | solution.py:234
  26.3 0.8 copy-start.1
  29.2 18.3 %all-to-all-start.1 = ((bf16[8,16,2048]{2,1,0:T(8,128)(2,1)}), bf16[8,16,2048]{2,1,0:T(8,128)(2,1)S(1)}, u32[]{:S(2)}, u32[]{:S(2)}) async-start(bf16[8,16,2048]{2,1,0:T(8,128)(2,1)} %get-tuple-element.20), calls=%async_computation.1 | async-start | bytes 1048576 | tf_op jit(solution)/shard_map/all_to_all | solution.py:283
  47.5 0.8 copy-start.3
  52.5 3.8 %collective-permute-start.1 = (f32[8,128]{1,0:T(8,128)}, f32[8,128]{1,0:T(8,128)S(1)}, u32[]{:S(2)}, u32[]{:S(2)}) collective-permute-start(f32[8,128]{1,0:T(8,128)} %get-tuple-element.23), channel_id=1, source_target_pairs={{0,2},{2,0},{1,3},{3,1},{4,6},{6,4},{5,7},{7,5},{8,10},{10,8},{9,1... | collective-permute-start | bytes 12296 | tf_op jit(solution)/shard_map/ppermute | solution.py:234
  61.6 18.6 %all-to-all-start.2 = ((bf16[8,16,2304]{2,1,0:T(8,128)(2,1)}), bf16[8,16,2304]{2,1,0:T(8,128)(2,1)S(1)}, u32[]{:S(2)}, u32[]{:S(2)}) async-start(bf16[8,16,2304]{2,1,0:T(8,128)(2,1)} %bitcast.35), calls=%async_computation.2 | async-start | bytes 1179648 | tf_op jit(solution)/shard_map/all_to_all | solution.py:296
  65.3 26.4 %copy-start.4 = (f32[128,1]{1,0:T(8,128)S(1)}, f32[128,1]{1,0:T(8,128)}, u32[]{:S(2)}) copy-start(f32[128,1]{1,0:T(8,128)} %get-tuple-element.25) | copy-start | bytes 1540
  80.2 0.8 copy-start
  83.1 17.7 %all-to-all-start.3 = ((bf16[8,16,2048]{2,1,0:T(8,128)(2,1)}), bf16[8,16,2048]{2,1,0:T(8,128)(2,1)S(1)}, u32[]{:S(2)}, u32[]{:S(2)}) async-start(bf16[8,16,2048]{2,1,0:T(8,128)(2,1)} %get-tuple-element.29), calls=%async_computation.3 | async-start | bytes 1048576 | tf_op jit(solution)/shard_map/all_to_all | solution.py:309
  86.8 7.4 %collective-permute-start.2 = (bf16[128,1024]{1,0:T(8,128)(2,1)S(1)}, bf16[128,1024]{1,0:T(8,128)(2,1)S(1)}, u32[]{:S(2)}, u32[]{:S(2)}) collective-permute-start(bf16[128,1024]{1,0:T(8,128)(2,1)S(1)} %select_convert_fusion), channel_id=1, source_target_pairs={{0,2},{2,0},{1,3},{3,1},{4,6},{6,4},{5,7},{7,5},{8,10},{10,8},{9,1... | collective-permute-start | bytes 786440 | tf_op jit(solution)/shard_map/ppermute | solution.py:234
  91.8 3.1 %collective-permute-start.3 = (f32[16,256]{1,0:T(8,128)}, f32[16,256]{1,0:T(8,128)S(1)}, u32[]{:S(2)}, u32[]{:S(2)}) collective-permute-start(f32[16,256]{1,0:T(8,128)} %get-tuple-element.33), channel_id=1, source_target_pairs={{0,1},{1,0},{2,3},{3,2},{4,5},{5,4},{6,7},{7,6},{8,9},{9,8},{10,11... | collective-permute-start | bytes 49160 | tf_op jit(solution)/shard_map/ppermute | solution.py:234
  100.8 0.8 copy-start.2
